TPU v7x, 32 devices: a whole 2x2x4 slice. The times are simulated.
32 devices in a mesh: lang: 8 (over z, core), batch: 4 (over y, x).
Axes of the slice: x: 2, y: 2, z: 4, core: 2. Of those that a mesh axis runs over, the one named last changes fastest.
Arguments:
- dec_states: bfloat16 [8, 48, 32, 1024], P('lang', 'batch'), may hold values from -6 to 6
- grad_out: bfloat16 [8, 48, 32, 1024], P('lang', 'batch'), may hold values from -6 to 6
- enc_rows: bfloat16 [8, 24, 128, 1024], P('lang', 'batch'), may hold values from -6 to 6
- source_lengths: int32 [8, 24], P('lang', 'batch'), may hold values from 1 to 128, as said below
- pair_counts: int32 [8, 8], replicated, may hold values from 0 to 2, as said below
- query_gain: float32 [8, 1024], P('lang'), may hold values from 0.5 to 1.5
- w_query: bfloat16 [8, 1024, 512], P('lang', 'batch'), may hold values from -0.1875 to 0.1875
- w_key: bfloat16 [8, 1024, 512], P('lang', 'batch'), may hold values from -0.1875 to 0.1875
- w_value: bfloat16 [8, 1024, 512], P('lang', 'batch'), may hold values from -0.1875 to 0.1875
- w_out: bfloat16 [8, 512, 1024], P('lang', 'batch'), may hold values from -0.25 to 0.25
Outputs:
- attended: bfloat16 [8, 48, 32, 1024], P('lang', 'batch')
- dec_grad: bfloat16 [8, 48, 32, 1024], P('lang', 'batch')
- enc_grad: bfloat16 [8, 24, 128, 1024], P('lang', 'batch')
- gain_grad: float32 [8, 1024], P('lang', 'batch')
- query_grad: float32 [8, 1024, 512], P('lang', 'batch')
- key_grad: float32 [8, 1024, 512], P('lang', 'batch')
- value_grad: float32 [8, 1024, 512], P('lang', 'batch')
- out_grad: float32 [8, 512, 1024], P('lang', 'batch')
Inputs may be any that keep to these rules, and one draw needn't show every extreme that they name: `pair_counts`: each row sums to 6; a device's sentences are ordered by target language; no column sums to more than 12 and some column sums to exactly 12; no entry exceeds 2, and some entry equals it. `source_lengths`: on every device some sentence has 128 real tokens and some has 1.
All inputs are finite; a program needn't handle non-finite values.
Results may differ from a plain program's by a relative error of at most 0.02.
Values may be sent and summed in bfloat16 or wider, within the bound.
No kernel may reach another device: no remote copies, remote signals or barrier semaphores. Data moves between devices by JAX's collectives and lax.ppermute only.
A program may use at most 128 MiB of HBM per device.

v0:
```python
import jax
import jax.numpy as jnp
from jax import lax
from jax.sharding import PartitionSpec as P

HEADS = 8
HDIM = 64


def cross_branch(states, query_gain, w_query, w_key, w_value, w_out, memory, key_lengths):
    slot_count = states.shape[0]
    states32 = states.astype(jnp.float32)
    scale_inv = lax.rsqrt(jnp.mean(states32 * states32, axis=-1, keepdims=True) + 1e-06)
    normed = (states32 * scale_inv * query_gain).astype(jnp.bfloat16)
    queries = jnp.einsum("ktd,de->kte", normed, w_query, preferred_element_type=jnp.float32).astype(
        jnp.bfloat16
    )
    key_rows = jnp.einsum("ksd,de->kse", memory, w_key, preferred_element_type=jnp.float32).astype(
        jnp.bfloat16
    )
    value_rows = jnp.einsum(
        "ksd,de->kse", memory, w_value, preferred_element_type=jnp.float32
    ).astype(jnp.bfloat16)
    queries = queries.reshape(slot_count, queries.shape[1], HEADS, HDIM)
    key_rows = key_rows.reshape(slot_count, key_rows.shape[1], HEADS, HDIM)
    value_rows = value_rows.reshape(slot_count, value_rows.shape[1], HEADS, HDIM)
    scores = jnp.einsum(
        "kthe,kshe->khts", queries, key_rows, preferred_element_type=jnp.float32
    ) * HDIM ** (-0.5)
    key_live = jnp.arange(key_rows.shape[1], dtype=jnp.int32)[None, :] < key_lengths[:, None]
    raised = jnp.where(key_live[:, None, None, :], jnp.exp(scores), 0.0)
    empty_slot = (key_lengths == 0).astype(jnp.float32)[:, None, None, None]
    shares = (raised / (jnp.sum(raised, axis=-1, keepdims=True) + empty_slot)).astype(jnp.bfloat16)
    context = jnp.einsum(
        "khts,kshe->kthe", shares, value_rows, preferred_element_type=jnp.float32
    ).astype(jnp.bfloat16)
    context = context.reshape(slot_count, context.shape[1], HEADS * HDIM)
    return jnp.einsum("kte,ed->ktd", context, w_out, preferred_element_type=jnp.float32)


def device_step(states, upstream, query_gain, w_query, w_key, w_value, w_out, memory, key_lengths):

    def branch_fn(states_in, gain_in, query_in, key_in, value_in, out_in, memory_in):
        return cross_branch(
            states_in, gain_in, query_in, key_in, value_in, out_in, memory_in, key_lengths
        )

    branch, backward = jax.vjp(
        branch_fn, states, query_gain, w_query, w_key, w_value, w_out, memory
    )
    gradients = backward(upstream.astype(jnp.float32))
    state_grad = (upstream.astype(jnp.float32) + gradients[0].astype(jnp.float32)).astype(
        jnp.bfloat16
    )
    return (branch.astype(jnp.bfloat16), state_grad, gradients[1:])


def per_device(
    dec_states,
    grad_out,
    enc_rows,
    source_lengths,
    pair_counts,
    query_gain,
    w_query,
    w_key,
    w_value,
    w_out,
):
    lang_count = lax.axis_size("lang")
    lang_index = lax.axis_index("lang")
    sent_count = enc_rows.shape[1]
    live_cap = dec_states.shape[1]
    pair_cap = (live_cap + lang_count - 1) // lang_count
    seq_len = enc_rows.shape[2]
    model_width = enc_rows.shape[3]
    full_query, full_key, full_value, full_out = (
        lax.all_gather(w_query, "batch", axis=1, tiled=True),
        lax.all_gather(w_key, "batch", axis=1, tiled=True),
        lax.all_gather(w_value, "batch", axis=1, tiled=True),
        lax.all_gather(w_out, "batch", axis=1, tiled=True),
    )
    send_counts = lax.dynamic_index_in_dim(pair_counts, lang_index, 0, keepdims=False)
    send_start = jnp.cumsum(send_counts) - send_counts
    pair_slots = jnp.arange(pair_cap, dtype=jnp.int32)[None, :]
    sending = pair_slots < send_counts[:, None]
    picked = jnp.clip(send_start[:, None] + pair_slots, 0, sent_count - 1)
    send_rows = jnp.where(
        sending[:, :, None, None], enc_rows[0][picked], jnp.zeros((), jnp.bfloat16)
    )
    send_lengths = jnp.where(sending, source_lengths[0][picked], 0).astype(jnp.bfloat16)
    got_rows, got_lengths = (
        lax.all_to_all(send_rows, "lang", split_axis=0, concat_axis=0, tiled=True),
        lax.all_to_all(send_lengths, "lang", split_axis=0, concat_axis=0, tiled=True),
    )
    recv_counts = lax.dynamic_index_in_dim(pair_counts, lang_index, 1, keepdims=False)
    recv_start = jnp.cumsum(recv_counts) - recv_counts
    slot_ids = jnp.arange(live_cap, dtype=jnp.int32)
    source_of = jnp.sum(
        (jnp.cumsum(recv_counts)[None, :] <= slot_ids[:, None]).astype(jnp.int32), axis=1
    )
    source_of = jnp.minimum(source_of, lang_count - 1)
    is_valid = slot_ids < jnp.sum(recv_counts)
    flat_slot = jnp.clip(
        source_of * pair_cap + slot_ids - recv_start[source_of], 0, lang_count * pair_cap - 1
    )
    got_flat = got_rows.reshape(lang_count * pair_cap, seq_len, model_width)
    memory = jnp.where(is_valid[:, None, None], got_flat[flat_slot], jnp.zeros((), jnp.bfloat16))
    key_lengths = jnp.where(
        is_valid, got_lengths.reshape(-1)[flat_slot].astype(jnp.float32), 0.0
    ).astype(jnp.int32)
    branch, state_grad, gradients = device_step(
        dec_states[0],
        grad_out[0],
        query_gain[0],
        full_query[0],
        full_key[0],
        full_value[0],
        full_out[0],
        memory,
        key_lengths,
    )
    gain_part, query_part, key_part, value_part, out_part, memory_grad = gradients
    back_slot = jnp.clip(recv_start[:, None] + pair_slots, 0, live_cap - 1)
    returning = pair_slots < recv_counts[:, None]
    back_rows = jnp.where(
        returning[:, :, None, None], memory_grad[back_slot], jnp.zeros((), jnp.bfloat16)
    )
    came_back = lax.all_to_all(back_rows, "lang", split_axis=0, concat_axis=0, tiled=True)
    sentence_ids = jnp.arange(sent_count, dtype=jnp.int32)
    target_of = jnp.sum(
        (jnp.cumsum(send_counts)[None, :] <= sentence_ids[:, None]).astype(jnp.int32), axis=1
    )
    back_index = target_of * pair_cap + sentence_ids - send_start[target_of]
    enc_grad = came_back.reshape(lang_count * pair_cap, seq_len, model_width)[back_index]
    summed = (
        lax.psum(query_part, "batch").astype(jnp.float32),
        lax.psum(key_part, "batch").astype(jnp.float32),
        lax.psum(value_part, "batch").astype(jnp.float32),
        lax.psum(out_part, "batch").astype(jnp.float32),
        lax.psum(gain_part.astype(jnp.bfloat16), "batch").astype(jnp.float32),
    )
    batch_count = lax.axis_size("batch")
    batch_index = lax.axis_index("batch")
    totals = tuple(
        (
            lax.dynamic_slice_in_dim(
                whole_sum,
                batch_index * (whole_sum.shape[0] // batch_count),
                whole_sum.shape[0] // batch_count,
                0,
            )
            for whole_sum in summed
        )
    )
    return (
        branch[None],
        state_grad[None],
        enc_grad[None],
        totals[4][None],
        totals[0][None],
        totals[1][None],
        totals[2][None],
        totals[3][None],
    )


def solution(mesh):
    return jax.shard_map(
        per_device,
        mesh=mesh,
        in_specs=(
            P("lang", "batch", None, None),
            P("lang", "batch", None, None),
            P("lang", "batch", None, None),
            P("lang", "batch"),
            P(),
            P("lang", None),
            P("lang", "batch", None),
            P("lang", "batch", None),
            P("lang", "batch", None),
            P("lang", "batch", None),
        ),
        out_specs=(
            P("lang", "batch", None, None),
            P("lang", "batch", None, None),
            P("lang", "batch", None, None),
            P("lang", "batch"),
            P("lang", "batch", None),
            P("lang", "batch", None),
            P("lang", "batch", None),
            P("lang", "batch", None),
        ),
        check_vma=False,
    )
```

profile of v0, /device:TPU:0, one launch (start us, length us, event | category | flops | bytes accessed | tf_op | source)
XLA Modules:
  0.0 305.7 jit_solution(16203825089451757280)
XLA Ops:
  11.2 6.4 %all-to-all-start.1 = ((bf16[8,1,2]{2,1,0:T(2,128)(2,1)}), bf16[8,1,2]{2,1,0:T(2,128)(2,1)S(1)}, u32[]{:S(2)}, u32[]{:S(2)}) async-start(bf16[8,1,2]{2,1,0:T(2,128)(2,1)} %copy.74), calls=%async_computation.1 | async-start | bytes 8192 | tf_op jit(solution)/shard_map/all_to_all | solution.py:94
  17.7 2.8 gather_fusion
  20.4 4.5 %broadcast_select_fusion.1 = bf16[8,2,128,1024]{3,2,1,0:T(8,128)(2,1)} fusion(bf16[8,2,128,1024]{3,2,1,0:T(8,128)(2,1)} %bitcast.170, pred[8,2]{1,0:T(8,128)(4,1)S(1)} %iota_compare_fusion.4), kind=kLoop, calls=%fused_computation.9 | loop fusion | flops 2097152 | bytes 8388624 | tf_op jit(solution)/shard_map/jit(_where)/select_n | solution.py:88
  24.9 5.2 %all-to-all-start = ((bf16[8,2,128,1024]{3,2,1,0:T(8,128)(2,1)}), bf16[8,2,128,1024]{3,2,1,0:T(8,128)(2,1)}, u32[]{:S(2)}, u32[]{:S(2)}) async-start(bf16[8,2,128,1024]{3,2,1,0:T(8,128)(2,1)} %broadcast_select_fusion.1), calls=%async_computation | async-start | bytes 8388608 | tf_op jit(solution)/shard_map/all_to_all | solution.py:93
  36.6 2.5 all-gather.7.cloned.1.call-done
  39.1 1.9 convolution_convert_fusion.10
  42.3 25.1 %all-gather.11.cloned.1.call-done = bf16[1,512,1024]{2,1,0:T(8,128)(2,1)} async-done(((bf16[1,128,1024]{2,1,0:T(8,128)(2,1)}), bf16[1,512,1024]{2,1,0:T(8,128)(2,1)}) %all-gather.11.cloned.1.call-update) | async-done | bytes 1048592 | tf_op jit(solution)/shard_map/all_gather | solution.py:81
  70.6 53.6 %all-to-all-done = bf16[8,2,128,1024]{3,2,1,0:T(8,128)(2,1)} async-done(((bf16[8,2,128,1024]{3,2,1,0:T(8,128)(2,1)}), bf16[8,2,128,1024]{3,2,1,0:T(8,128)(2,1)}, u32[]{:S(2)}, u32[]{:S(2)}) %all-to-all-start) | async-done | bytes 4194336 | tf_op jit(solution)/shard_map/all_to_all | solution.py:93
  124.2 4.7 %gather_fusion.2 = bf16[12,128,1024]{2,1,0:T(8,128)(2,1)} fusion(bf16[16,128,1024]{2,1,0:T(8,128)(2,1)} %bitcast.5, s32[1024]{0:T(1024)S(1)} %pad_clamp_fusion.3), kind=kCustom, calls=%fused_computation.2 | custom fusion | bytes 6291504 | tf_op jit(solution)/shard_map/gather | solution.py:108
  129.0 4.0 %convolution_convert_fusion.2 = bf16[12,128,512]{2,1,0:T(8,128)(2,1)S(1)} fusion(bf16[1,1024,512]{2,1,0:T(8,128)(2,1)} %all-gather.9.cloned.1.call-done, bf16[12,128,1024]{2,1,0:T(8,128)(2,1)} %gather_fusion.2, pred[12]{0:T(512)(128)(4,1)S(1)} %iota_compare_fusion.5), kind=kOutput, calls=%fused_computation.30 | convolution fusion | flops 1612972032 | bytes 5767180 | tf_op jit(solution)/shard_map/jvp(ksd,de->kse)/dot_general | solution.py:18
  134.1 4.0 %convolution_convert_fusion.3 = bf16[12,128,512]{2,1,0:T(8,128)(2,1)S(1)} fusion(bf16[1,1024,512]{2,1,0:T(8,128)(2,1)} %all-gather.5.cloned.1.call-done, bf16[12,128,1024]{2,1,0:T(8,128)(2,1)} %gather_fusion.2, pred[12]{0:T(512)(128)(4,1)S(1)} %iota_compare_fusion.5), kind=kOutput, calls=%fused_computation.31 | convolution fusion | flops 1612972032 | bytes 5767180 | tf_op jit(solution)/shard_map/jvp(ksd,de->kse)/dot_general | solution.py:21
  147.8 3.5 %convert_add_fusion = bf16[12,128,1024]{2,1,0:T(8,128)(2,1)} fusion(bf16[12,128,1024]{2,1,0:T(8,128)(2,1)S(1)} %fusion.26, bf16[12,128,512]{1,2,0:T(8,128)(2,1)S(1)} %bitcast.184, bf16[1,1024,512]{2,1,0:T(8,128)(2,1)S(1)} %copy-done.21), kind=kOutput, calls=%fused_computation.10 | convolution fusion | flops 1613758464 | bytes 8912896 | tf_op jit(solution)/shard_map/transpose(jvp(ksd,de->kse))/dot_general | solution.py:18
  151.3 4.7 %gather_fusion.5 = bf16[16,128,1024]{2,1,0:T(8,128)(2,1)} fusion(bf16[12,128,1024]{2,1,0:T(8,128)(2,1)} %convert_add_fusion, s32[1024]{0:T(1024)S(1)} %pad_clamp_fusion.2), kind=kCustom, calls=%fused_computation.5 | custom fusion | bytes 8388672 | tf_op jit(solution)/shard_map/gather | solution.py:127
  156.0 4.5 %broadcast_select_fusion = bf16[8,2,128,1024]{3,2,1,0:T(8,128)(2,1)} fusion(bf16[8,2,128,1024]{3,2,1,0:T(8,128)(2,1)} %bitcast.169, pred[8,2]{1,0:T(8,128)(4,1)S(1)} %iota_compare_fusion.2), kind=kLoop, calls=%fused_computation.8 | loop fusion | flops 2097152 | bytes 8388624 | tf_op jit(solution)/shard_map/jit(_where)/select_n | solution.py:126
  160.5 4.6 %all-to-all-start.2 = ((bf16[8,2,128,1024]{3,2,1,0:T(8,128)(2,1)}), bf16[8,2,128,1024]{3,2,1,0:T(8,128)(2,1)}, u32[]{:S(2)}, u32[]{:S(2)}) async-start(bf16[8,2,128,1024]{3,2,1,0:T(8,128)(2,1)} %broadcast_select_fusion), calls=%async_computation.2 | async-start | bytes 8388608 | tf_op jit(solution)/shard_map/all_to_all | solution.py:129
  165.1 2.2 fusion.17
  177.7 3.1 %bitcast_convert_fusion.2 = bf16[1024,512]{1,0:T(8,128)(2,1)} fusion(bf16[12,128,512]{1,2,0:T(8,128)(2,1)S(1)} %bitcast.185, bf16[12,128,1024]{2,1,0:T(8,128)(2,1)S(1)} %copy-done.6, pred[12]{0:T(512)(128)(4,1)S(1)} %copy-done.28), kind=kOutput, calls=%fused_computation.15 | convolution fusion | flops 1612709888 | bytes 5767180 | tf_op jit(solution)/shard_map/transpose(jvp(ksd,de->kse))/dot_general | solution.py:18
  180.8 3.1 %bitcast_convert_fusion.1 = bf16[1024,512]{1,0:T(8,128)(2,1)} fusion(bf16[12,128,512]{1,2,0:T(8,128)(2,1)S(1)} %bitcast.183, bf16[12,128,1024]{2,1,0:T(8,128)(2,1)S(1)} %copy-done.6, pred[12]{0:T(512)(128)(4,1)S(1)} %copy-done.28), kind=kOutput, calls=%fused_computation.14 | convolution fusion | flops 1612709888 | bytes 5767180 | tf_op jit(solution)/shard_map/transpose(jvp(ksd,de->kse))/dot_general | solution.py:21
  185.3 2.1 fusion.15
  187.4 10.4 %psum.35 = bf16[1024]{0:T(1024)(128)(2,1)S(1)} all-reduce(bf16[1024]{0:T(1024)(128)(2,1)S(1)} %get-tuple-element.8), channel_id=1, replica_groups=mesh['lang'=8,'batch'=4] {'batch'}, use_global_device_ids=true, to_apply=%region_10.11 | all-reduce | flops 1024 | bytes 4096 | tf_op jit(solution)/shard_map/psum | solution.py:141
  198.4 2.7 fusion.18
  202.5 86.7 %all-reduce.3.cloned.1.call-done = (bf16[1024,512]{1,0:T(8,128)(2,1)}, bf16[1024,512]{1,0:T(8,128)(2,1)}, bf16[1024,512]{1,0:T(8,128)(2,1)}, bf16[512,1024]{1,0:T(8,128)(2,1)}) async-done(((bf16[1024,512]{1,0:T(8,128)(2,1)}, bf16[1024,512]{1,0:T(8,128)(2,1)}, bf16[1024,512]{1,0:T(8,128)(2,1)}, bf16[512,1024]{1,0:T(8,128)(2,1)}), (bf16[1024,512]{1,0:T(8,128)(2,1)}, bf16[1024,512]{1,0:T(8,128)(2,1)}, ...) | async-done | bytes 4194320 | tf_op jit(solution)/shard_map/psum | solution.py:137
  292.8 2.1 convert_bitcast_fusion.2
  295.0 4.1 %gather_fusion.7 = bf16[6,128,1024]{2,1,0:T(8,128)(2,1)} fusion(bf16[16,128,1024]{2,1,0:T(8,128)(2,1)} %bitcast.35, s32[1024]{0:T(1024)S(1)} %pad_clamp_fusion), kind=kCustom, calls=%fused_computation.7 | custom fusion | bytes 3145752 | tf_op jit(solution)/shard_map/gather | solution.py:135
  (136 shorter events, 42.9 us)
Async XLA Ops:
  7.2 10.5 %copy-start = (bf16[1,6,128,1024]{3,2,1,0:T(8,128)(2,1)S(1)}, bf16[1,6,128,1024]{3,2,1,0:T(8,128)(2,1)}, u32[]{:S(2)}) copy-start(bf16[1,6,128,1024]{3,2,1,0:T(8,128)(2,1)} %param.12) | copy-start | bytes 4718596
  7.2 2.5 copy-start.2
  7.2 31.9 %all-gather.7.cloned.1.call-start = ((), (), s32[]{:S(2)}) async-start(), calls=%async_computation.4 | async-start | bytes 1310720 | tf_op jit(solution)/shard_map/all_gather | solution.py:78
  11.2 13.7 %all-to-all-start.1 = ((bf16[8,1,2]{2,1,0:T(2,128)(2,1)}), bf16[8,1,2]{2,1,0:T(2,128)(2,1)S(1)}, u32[]{:S(2)}, u32[]{:S(2)}) async-start(bf16[8,1,2]{2,1,0:T(2,128)(2,1)} %copy.74), calls=%async_computation.1 | async-start | bytes 8192 | tf_op jit(solution)/shard_map/all_to_all | solution.py:94
  24.9 7.3 %copy-start.16 = (s32[8,8]{1,0:T(8,128)S(1)}, s32[8,8]{1,0:T(8,128)}, u32[]{:S(2)}) copy-start(s32[8,8]{1,0:T(8,128)} %param.14) | copy-start | bytes 772
  24.9 99.3 %all-to-all-start = ((bf16[8,2,128,1024]{3,2,1,0:T(8,128)(2,1)}), bf16[8,2,128,1024]{3,2,1,0:T(8,128)(2,1)}, u32[]{:S(2)}, u32[]{:S(2)}) async-start(bf16[8,2,128,1024]{3,2,1,0:T(8,128)(2,1)} %broadcast_select_fusion.1), calls=%async_computation | async-start | bytes 8388608 | tf_op jit(solution)/shard_map/all_to_all | solution.py:93
  30.1 3.9 %copy-start.7 = (bf16[1,12,32,1024]{3,2,1,0:T(8,128)(2,1)S(1)}, bf16[1,12,32,1024]{3,2,1,0:T(8,128)(2,1)}, u32[]{:S(2)}) copy-start(bf16[1,12,32,1024]{3,2,1,0:T(8,128)(2,1)} %param.10) | copy-start | bytes 2359300
  30.2 9.0 %copy-start.17 = (f32[1,1024]{1,0:T(1,128)S(1)}, f32[1,1024]{1,0:T(1,128)}, u32[]{:S(2)}) copy-start(f32[1,1024]{1,0:T(1,128)} %param.15) | copy-start | bytes 12292
  30.2 37.3 %all-gather.11.cloned.1.call-start = ((), (), s32[]{:S(2)}) async-start(), calls=%async_computation.6 | async-start | bytes 1310720 | tf_op jit(solution)/shard_map/all_gather | solution.py:81
  30.9 98.1 %all-gather.9.cloned.1.call-start = ((), (), s32[]{:S(2)}) async-start(), calls=%async_computation.5 | async-start | bytes 1310720 | tf_op jit(solution)/shard_map/all_gather | solution.py:79
  31.6 102.5 %all-gather.5.cloned.1.call-start = ((), (), s32[]{:S(2)}) async-start(), calls=%async_computation.3 | async-start | bytes 1310720 | tf_op jit(solution)/shard_map/all_gather | solution.py:80
  34.4 6.7 %copy-start.14 = (f32[12,32]{1,0:T(8,128)}, f32[12,32]{1,0:T(8,128)S(1)}, u32[]{:S(2)}) copy-start(f32[12,32]{1,0:T(8,128)S(1)} %fusion.41) | copy-start | bytes 4612
  35.0 99.1 %copy-start.27 = (pred[12]{0:T(512)(128)(4,1)}, pred[12]{0:T(512)(128)(4,1)S(1)}, u32[]{:S(2)}) copy-start(pred[12]{0:T(512)(128)(4,1)S(1)} %iota_compare_fusion.5) | copy-start | bytes 40
  39.1 28.4 %copy-start.10 = (bf16[1,12,32,1024]{3,2,1,0:T(8,128)(2,1)S(1)}, bf16[1,12,32,1024]{3,2,1,0:T(8,128)(2,1)}, u32[]{:S(2)}) copy-start(bf16[1,12,32,1024]{3,2,1,0:T(8,128)(2,1)} %param.11) | copy-start | bytes 2359300
  139.7 2.0 copy-start.3
  139.7 2.0 copy-start.9
  141.7 23.4 %copy-start.13 = (f32[12,8,32]{2,1,0:T(8,128)}, f32[12,8,32]{2,1,0:T(8,128)S(1)}, u32[]{:S(2)}) copy-start(f32[12,8,32]{2,1,0:T(8,128)S(1)} %get-tuple-element.19) | copy-start | bytes 36868
  160.5 134.5 %all-to-all-start.2 = ((bf16[8,2,128,1024]{3,2,1,0:T(8,128)(2,1)}), bf16[8,2,128,1024]{3,2,1,0:T(8,128)(2,1)}, u32[]{:S(2)}, u32[]{:S(2)}) async-start(bf16[8,2,128,1024]{3,2,1,0:T(8,128)(2,1)} %broadcast_select_fusion), calls=%async_computation.2 | async-start | bytes 8388608 | tf_op jit(solution)/shard_map/all_to_all | solution.py:129
  165.0 124.2 %all-reduce.3.cloned.1.call-start = ((), (), s32[]{:S(2)}) async-start(), calls=%async_computation.7 | async-start | bytes 8388608 | tf_op jit(solution)/shard_map/psum | solution.py:137
  167.3 3.0 copy-start.4
  174.9 2.7 copy-start.26
  174.9 2.7 copy-start.28
  177.7 3.1 %copy-start.24 = (bf16[12,8,64,128]{3,2,1,0:T(8,128)(2,1)S(1)}, bf16[12,8,64,128]{3,2,1,0:T(8,128)(2,1)}, u32[]{:S(2)}) copy-start(bf16[12,8,64,128]{3,2,1,0:T(8,128)(2,1)} %copy-done.23) | copy-start | bytes 4718596
  295.0 4.2 %copy-start.1 = (bf16[1,6,128,1024]{3,2,1,0:T(8,128)(2,1)S(1)}, bf16[1,6,128,1024]{3,2,1,0:T(8,128)(2,1)}, u32[]{:S(2)}) copy-start(bf16[1,6,128,1024]{3,2,1,0:T(8,128)(2,1)} %param.12) | copy-start | bytes 4718596
  (13 other events, 19.8 us)
Sparse Core Ops, SparseCore 0:
  9.8 29.2 all-gather.6
  40.9 26.4 all-gather.10
  69.3 26.4 all-gather.8
  97.5 26.4 all-gather.4
  184.0 105.1 all-reduce.2
where the time goes:
time: 307 us; the launch traced here: 306 us
  waiting for transfers between devices  171 us (56%)
  matrix products  41.3 us (13%)
  local copies, waits for them, and re-layouts  32.6 us (11%)
  other arithmetic  20.1 us (7%)
  starting transfers between devices  16.3 us (5%)
  between operations  14.2 us (5%)
  blocking collectives  10.4 us (3%)
    psum x1, waiting for transfers between devices, per_device(): lax.psum(query_part, 'batch').astype(jnp.float32)  86.7 us
    all_to_all x1, waiting for transfers between devices, per_device(): lax.all_to_all(send_rows, 'lang', split_axis=0, concat_axis=0, tiled=True)  53.6 us
    all_gather x1, waiting for transfers between devices, per_device(): lax.all_gather(w_out, 'batch', axis=1, tiled=True)  25.1 us
    dot_general x3, matrix products, cross_branch(): jnp.einsum('ksd,de->kse', memory, w_key, preferred_element_type=jnp.float32)  10.6 us
    psum x1, blocking collectives, per_device(): lax.psum(gain_part.astype(jnp.bfloat16), 'batch').astype(jnp.float32)  10.4 us
    dot_general x3, matrix products, cross_branch(): jnp.einsum('ksd,de->kse', memory, w_value, preferred_element_type=jnp.flo...  9 us
    all_to_all x1, starting transfers between devices, per_device(): lax.all_to_all(send_lengths, 'lang', split_axis=0, concat_axis=0, tiled=T...  6.35 us
    dot_general x3, matrix products, cross_branch(): jnp.einsum('kte,ed->ktd', context, w_out, preferred_element_type=jnp.floa...  6.26 us
  transfers between devices with their start and end apart: 8, of which 4 were waited for; matrix products, arithmetic and copies ran while one was open for 20% of the time, Pallas kernels for 0%

commit v1 on v0

--- a/solution.py
+++ b/solution.py
@@ -134,7 +134,7 @@
     back_index = target_of * pair_cap + sentence_ids - send_start[target_of]
     enc_grad = came_back.reshape(lang_count * pair_cap, seq_len, model_width)[back_index]
     summed = (
-        lax.psum(query_part, "batch").astype(jnp.float32),
+        jnp.sum(lax.all_gather(query_part, "batch"), axis=0).astype(jnp.float32),
         lax.psum(key_part, "batch").astype(jnp.float32),
         lax.psum(value_part, "batch").astype(jnp.float32),
         lax.psum(out_part, "batch").astype(jnp.float32),

time: 307 us -> 331 us (1.078)
  waiting for transfers between devices: 171 us -> 183 us
  other arithmetic: 20.1 us -> 27 us
  matrix products: 41.3 us -> 46 us
    all_gather x0 -> x1, waiting for transfers between devices: none -> 51 us  [per_device(): lax.all_gather(query_part, 'batch')]
    psum x1, waiting for transfers between devices: 86.7 us -> 37.9 us  [per_device(): lax.psum(key_part, 'batch').astype(jnp.float32)]
    all_to_all x1, waiting for transfers between devices: 53.6 us -> 31.9 us  [per_device(): lax.all_to_all(send_rows, 'lang', split_axis=0, concat_axis=0, tiled=True)]
    all_gather x1, waiting for transfers between devices: 2.54 us -> 23.1 us  [per_device(): lax.all_gather(w_query, 'batch', axis=1, tiled=True)]
    all_gather x1, waiting for transfers between devices: 0.02 us -> 11.8 us  [per_device(): lax.all_gather(w_value, 'batch', axis=1, tiled=True)]
    reduce_sum x0 -> x1, other arithmetic: none -> 3.5 us  [per_device(): jnp.sum(lax.all_gather(query_part, 'batch'), axis=0).astype(jnp.float32)]
  transfers between devices with their start and end apart: 8 -> 9, of which waited for: 4 -> 6; matrix products, arithmetic and copies ran while one was open for 20% -> 21% of each run, Pallas kernels for 0% -> 0%
where the time goes in v1:
time: 331 us; the launch traced here: 330 us
  waiting for transfers between devices  183 us (55%)
  matrix products  46 us (14%)
  local copies, waits for them, and re-layouts  33 us (10%)
  other arithmetic  27 us (8%)
  starting transfers between devices  16.6 us (5%)
  between operations  14.6 us (4%)
  blocking collectives  9.38 us (3%)
    all_gather x1, waiting for transfers between devices, per_device(): lax.all_gather(query_part, 'batch')  51 us
    psum x1, waiting for transfers between devices, per_device(): lax.psum(key_part, 'batch').astype(jnp.float32)  37.9 us
    all_to_all x1, waiting for transfers between devices, per_device(): lax.all_to_all(send_rows, 'lang', split_axis=0, concat_axis=0, tiled=True)  31.9 us
    all_gather x1, waiting for transfers between devices, per_device(): lax.all_gather(w_out, 'batch', axis=1, tiled=True)  25.1 us
    all_gather x1, waiting for transfers between devices, per_device(): lax.all_gather(w_query, 'batch', axis=1, tiled=True)  23.1 us
    all_gather x1, waiting for transfers between devices, per_device(): lax.all_gather(w_value, 'batch', axis=1, tiled=True)  11.8 us
    dot_general x3, matrix products, cross_branch(): jnp.einsum('ksd,de->kse', memory, w_value, preferred_element_type=jnp.flo...  11.4 us
    dot_general x3, matrix products, cross_branch(): jnp.einsum('ksd,de->kse', memory, w_key, preferred_element_type=jnp.float32)  10.6 us
  transfers between devices with their start and end apart: 9, of which 6 were waited for; matrix products, arithmetic and copies ran while one was open for 21% of the time, Pallas kernels for 0%

profile of v1, /device:TPU:0, one launch (start us, length us, event | category | flops | bytes accessed | tf_op | source)
XLA Modules:
  0.0 330.0 jit_solution(13745895144313602420)
XLA Ops:
  10.6 6.4 %all-to-all-start.1 = ((bf16[8,1,2]{2,1,0:T(2,128)(2,1)}), bf16[8,1,2]{2,1,0:T(2,128)(2,1)S(1)}, u32[]{:S(2)}, u32[]{:S(2)}) async-start(bf16[8,1,2]{2,1,0:T(2,128)(2,1)} %copy.74), calls=%async_computation.1 | async-start | bytes 8192 | tf_op jit(solution)/shard_map/all_to_all | solution.py:94
  17.0 2.8 gather_fusion
  19.8 4.5 %broadcast_select_fusion.1 = bf16[8,2,128,1024]{3,2,1,0:T(8,128)(2,1)} fusion(bf16[8,2,128,1024]{3,2,1,0:T(8,128)(2,1)} %bitcast.171, pred[8,2]{1,0:T(8,128)(4,1)S(1)} %iota_compare_fusion.4), kind=kLoop, calls=%fused_computation.9 | loop fusion | flops 2097152 | bytes 8388624 | tf_op jit(solution)/shard_map/jit(_where)/select_n | solution.py:88
  24.3 5.2 %all-to-all-start = ((bf16[8,2,128,1024]{3,2,1,0:T(8,128)(2,1)}), bf16[8,2,128,1024]{3,2,1,0:T(8,128)(2,1)}, u32[]{:S(2)}, u32[]{:S(2)}) async-start(bf16[8,2,128,1024]{3,2,1,0:T(8,128)(2,1)} %broadcast_select_fusion.1), calls=%async_computation | async-start | bytes 8388608 | tf_op jit(solution)/shard_map/all_to_all | solution.py:93
  37.1 23.1 %all-gather.9.cloned.1.call-done = bf16[1,1024,512]{2,1,0:T(8,128)(2,1)} async-done(((bf16[1,256,512]{2,1,0:T(8,128)(2,1)}), bf16[1,1024,512]{2,1,0:T(8,128)(2,1)}) %all-gather.9.cloned.1.call-update) | async-done | bytes 1048592 | tf_op jit(solution)/shard_map/all_gather | solution.py:78
  63.4 25.1 %all-gather.13.cloned.1.call-done = bf16[1,512,1024]{2,1,0:T(8,128)(2,1)} async-done(((bf16[1,128,1024]{2,1,0:T(8,128)(2,1)}), bf16[1,512,1024]{2,1,0:T(8,128)(2,1)}) %all-gather.13.cloned.1.call-update) | async-done | bytes 1048592 | tf_op jit(solution)/shard_map/all_gather | solution.py:81
  91.7 31.9 %all-to-all-done = bf16[8,2,128,1024]{3,2,1,0:T(8,128)(2,1)} async-done(((bf16[8,2,128,1024]{3,2,1,0:T(8,128)(2,1)}), bf16[8,2,128,1024]{3,2,1,0:T(8,128)(2,1)}, u32[]{:S(2)}, u32[]{:S(2)}) %all-to-all-start) | async-done | bytes 4194336 | tf_op jit(solution)/shard_map/all_to_all | solution.py:93
  123.6 4.8 %gather_fusion.2 = bf16[12,128,1024]{2,1,0:T(8,128)(2,1)} fusion(bf16[16,128,1024]{2,1,0:T(8,128)(2,1)} %bitcast.5, s32[1024]{0:T(1024)S(1)} %pad_clamp_fusion.3), kind=kCustom, calls=%fused_computation.2 | custom fusion | bytes 6291504 | tf_op jit(solution)/shard_map/gather | solution.py:108
  128.4 4.0 %convolution_convert_fusion.2 = bf16[12,128,512]{2,1,0:T(8,128)(2,1)S(1)} fusion(bf16[1,1024,512]{2,1,0:T(8,128)(2,1)} %all-gather.11.cloned.1.call-done, bf16[12,128,1024]{2,1,0:T(8,128)(2,1)} %gather_fusion.2, pred[12]{0:T(512)(128)(4,1)S(1)} %iota_compare_fusion.5), kind=kOutput, calls=%fused_computation.30 | convolution fusion | flops 1612972032 | bytes 5767180 | tf_op jit(solution)/shard_map/jvp(ksd,de->kse)/dot_general | solution.py:18
  133.4 11.8 %all-gather.7.cloned.1.call-done = bf16[1,1024,512]{2,1,0:T(8,128)(2,1)} async-done(((bf16[1,256,512]{2,1,0:T(8,128)(2,1)}), bf16[1,1024,512]{2,1,0:T(8,128)(2,1)}) %all-gather.7.cloned.1.call-update) | async-done | bytes 1048592 | tf_op jit(solution)/shard_map/all_gather | solution.py:80
  145.2 4.0 %convolution_convert_fusion.3 = bf16[12,128,512]{2,1,0:T(8,128)(2,1)S(1)} fusion(bf16[1,1024,512]{2,1,0:T(8,128)(2,1)} %all-gather.7.cloned.1.call-done, bf16[12,128,1024]{2,1,0:T(8,128)(2,1)} %gather_fusion.2, pred[12]{0:T(512)(128)(4,1)S(1)} %iota_compare_fusion.5), kind=kOutput, calls=%fused_computation.31 | convolution fusion | flops 1612972032 | bytes 5767180 | tf_op jit(solution)/shard_map/jvp(ksd,de->kse)/dot_general | solution.py:21
  161.2 3.0 bitcast_convert_fusion
  166.2 3.1 bitcast_convert_fusion.2
  169.3 3.1 bitcast_convert_fusion.1
  177.6 4.3 %fusion.26 = bf16[12,128,1024]{2,1,0:T(8,128)(2,1)S(1)} fusion(bf16[12,128,512]{1,2,0:T(8,128)(2,1)} %bitcast.184, bf16[1,1024,512]{2,1,0:T(8,128)(2,1)} %all-gather.7.cloned.1.call-done), kind=kOutput, calls=%fused_computation.64 | convolution fusion | flops 1610612736 | bytes 5767168 | tf_op jit(solution)/shard_map/transpose(jvp(ksd,de->kse))/dot_general | solution.py:21
  181.9 3.5 %convert_add_fusion = bf16[12,128,1024]{2,1,0:T(8,128)(2,1)} fusion(bf16[12,128,1024]{2,1,0:T(8,128)(2,1)S(1)} %fusion.26, bf16[12,128,512]{1,2,0:T(8,128)(2,1)S(1)} %bitcast.187, bf16[1,1024,512]{2,1,0:T(8,128)(2,1)S(1)} %copy-done.23), kind=kOutput, calls=%fused_computation.10 | convolution fusion | flops 1613758464 | bytes 8912896 | tf_op jit(solution)/shard_map/transpose(jvp(ksd,de->kse))/dot_general | solution.py:18
  185.4 4.9 %gather_fusion.5 = bf16[16,128,1024]{2,1,0:T(8,128)(2,1)} fusion(bf16[12,128,1024]{2,1,0:T(8,128)(2,1)} %convert_add_fusion, s32[1024]{0:T(1024)} %pad_clamp_fusion.2), kind=kCustom, calls=%fused_computation.5 | custom fusion | bytes 8388672 | tf_op jit(solution)/shard_map/gather | solution.py:127
  190.3 4.5 %broadcast_select_fusion = bf16[8,2,128,1024]{3,2,1,0:T(8,128)(2,1)} fusion(bf16[8,2,128,1024]{3,2,1,0:T(8,128)(2,1)} %bitcast.170, pred[8,2]{1,0:T(8,128)(4,1)} %iota_compare_fusion.2), kind=kLoop, calls=%fused_computation.8 | loop fusion | flops 2097152 | bytes 8388624 | tf_op jit(solution)/shard_map/jit(_where)/select_n | solution.py:126
  194.8 4.8 %all-to-all-start.2 = ((bf16[8,2,128,1024]{3,2,1,0:T(8,128)(2,1)}), bf16[8,2,128,1024]{3,2,1,0:T(8,128)(2,1)}, u32[]{:S(2)}, u32[]{:S(2)}) async-start(bf16[8,2,128,1024]{3,2,1,0:T(8,128)(2,1)} %broadcast_select_fusion), calls=%async_computation.2 | async-start | bytes 8388608 | tf_op jit(solution)/shard_map/all_to_all | solution.py:129
  207.7 9.4 %psum.28 = bf16[1024]{0:T(1024)(128)(2,1)S(1)} all-reduce(bf16[1024]{0:T(1024)(128)(2,1)S(1)} %get-tuple-element.8), channel_id=1, replica_groups=mesh['lang'=8,'batch'=4] {'batch'}, use_global_device_ids=true, to_apply=%region_10.11 | all-reduce | flops 1024 | bytes 4096 | tf_op jit(solution)/shard_map/psum | solution.py:141
  221.9 37.9 %all-reduce.3.cloned.1.call-done = (bf16[1024,512]{1,0:T(8,128)(2,1)}, bf16[1024,512]{1,0:T(8,128)(2,1)}, bf16[512,1024]{1,0:T(8,128)(2,1)}) async-done(((bf16[1024,512]{1,0:T(8,128)(2,1)}, bf16[1024,512]{1,0:T(8,128)(2,1)}, bf16[512,1024]{1,0:T(8,128)(2,1)}), (bf16[1024,512]{1,0:T(8,128)(2,1)}, bf16[1024,512]{1,0:T(8,128)(2,1)}, bf16[512,1024]{1,0:T(8,128)(2,1)})) %all-reduce.3.cloned.1.call-update) | async-done | bytes 3145744 | tf_op jit(solution)/shard_map/psum | solution.py:138
  263.7 51.0 %all-gather.15.cloned.1.call-done = bf16[4096,512]{1,0:T(8,128)(2,1)} async-done(((bf16[1024,512]{1,0:T(8,128)(2,1)}), bf16[4096,512]{1,0:T(8,128)(2,1)}) %all-gather.15.cloned.1.call-update) | async-done | bytes 4194320 | tf_op jit(solution)/shard_map/all_gather | solution.py:137
  314.7 3.5 %reduce_sum.107 = bf16[1024,512]{1,0:T(8,128)(2,1)S(1)} reduce(bf16[4,1024,512]{2,1,0:T(8,128)(2,1)} %bitcast.176, bf16[]{:T(256)} %constant.30.clone.1), dimensions={0}, to_apply=%region_11.12 | reduce | flops 1572864 | bytes 5242882 | tf_op jit(solution)/shard_map/reduce_sum | solution.py:137
  319.0 4.1 %gather_fusion.7 = bf16[6,128,1024]{2,1,0:T(8,128)(2,1)} fusion(bf16[16,128,1024]{2,1,0:T(8,128)(2,1)} %bitcast.35, s32[1024]{0:T(1024)S(1)} %pad_clamp_fusion), kind=kCustom, calls=%fused_computation.7 | custom fusion | bytes 3145752 | tf_op jit(solution)/shard_map/gather | solution.py:135
  (140 shorter events, 54.7 us)
Async XLA Ops:
  7.2 9.9 %copy-start = (bf16[1,6,128,1024]{3,2,1,0:T(8,128)(2,1)S(1)}, bf16[1,6,128,1024]{3,2,1,0:T(8,128)(2,1)}, u32[]{:S(2)}) copy-start(bf16[1,6,128,1024]{3,2,1,0:T(8,128)(2,1)} %param.12) | copy-start | bytes 4718596
  10.6 13.7 %all-to-all-start.1 = ((bf16[8,1,2]{2,1,0:T(2,128)(2,1)}), bf16[8,1,2]{2,1,0:T(2,128)(2,1)S(1)}, u32[]{:S(2)}, u32[]{:S(2)}) async-start(bf16[8,1,2]{2,1,0:T(2,128)(2,1)} %copy.74), calls=%async_computation.1 | async-start | bytes 8192 | tf_op jit(solution)/shard_map/all_to_all | solution.py:94
  24.3 8.1 %copy-start.17 = (s32[8,8]{1,0:T(8,128)S(1)}, s32[8,8]{1,0:T(8,128)}, u32[]{:S(2)}) copy-start(s32[8,8]{1,0:T(8,128)} %param.14) | copy-start | bytes 772
  24.3 99.3 %all-to-all-start = ((bf16[8,2,128,1024]{3,2,1,0:T(8,128)(2,1)}), bf16[8,2,128,1024]{3,2,1,0:T(8,128)(2,1)}, u32[]{:S(2)}, u32[]{:S(2)}) async-start(bf16[8,2,128,1024]{3,2,1,0:T(8,128)(2,1)} %broadcast_select_fusion.1), calls=%async_computation | async-start | bytes 8388608 | tf_op jit(solution)/shard_map/all_to_all | solution.py:93
  29.5 5.1 %copy-start.6 = (bf16[1,12,32,1024]{3,2,1,0:T(8,128)(2,1)S(1)}, bf16[1,12,32,1024]{3,2,1,0:T(8,128)(2,1)}, u32[]{:S(2)}) copy-start(bf16[1,12,32,1024]{3,2,1,0:T(8,128)(2,1)} %param.10) | copy-start | bytes 2359300
  29.5 30.7 %copy-start.18 = (f32[1,1024]{1,0:T(1,128)S(1)}, f32[1,1024]{1,0:T(1,128)}, u32[]{:S(2)}) copy-start(f32[1,1024]{1,0:T(1,128)} %param.15) | copy-start | bytes 12292
  29.5 30.6 %all-gather.9.cloned.1.call-start = ((), (), s32[]{:S(2)}) async-start(), calls=%async_computation.4 | async-start | bytes 1310720 | tf_op jit(solution)/shard_map/all_gather | solution.py:78
  30.3 58.3 %all-gather.13.cloned.1.call-start = ((), (), s32[]{:S(2)}) async-start(), calls=%async_computation.6 | async-start | bytes 1310720 | tf_op jit(solution)/shard_map/all_gather | solution.py:81
  31.0 97.4 %all-gather.11.cloned.1.call-start = ((), (), s32[]{:S(2)}) async-start(), calls=%async_computation.5 | async-start | bytes 1310720 | tf_op jit(solution)/shard_map/all_gather | solution.py:79
  31.8 113.4 %all-gather.7.cloned.1.call-start = ((), (), s32[]{:S(2)}) async-start(), calls=%async_computation.3 | async-start | bytes 1310720 | tf_op jit(solution)/shard_map/all_gather | solution.py:80
  32.3 227.5 %all-reduce.3.cloned.1.call-start = ((), (), s32[]{:S(2)}) async-start(), calls=%async_computation.8 | async-start | bytes 6291456 | tf_op jit(solution)/shard_map/psum | solution.py:138
  34.9 27.2 %copy-start.15 = (f32[12,32]{1,0:T(8,128)}, f32[12,32]{1,0:T(8,128)S(1)}, u32[]{:S(2)}) copy-start(f32[12,32]{1,0:T(8,128)S(1)} %fusion.41) | copy-start | bytes 4612
  35.5 109.6 %copy-start.27 = (pred[12]{0:T(512)(128)(4,1)}, pred[12]{0:T(512)(128)(4,1)S(1)}, u32[]{:S(2)}) copy-start(pred[12]{0:T(512)(128)(4,1)S(1)} %iota_compare_fusion.5) | copy-start | bytes 40
  60.2 28.4 %copy-start.9 = (bf16[1,12,32,1024]{3,2,1,0:T(8,128)(2,1)S(1)}, bf16[1,12,32,1024]{3,2,1,0:T(8,128)(2,1)}, u32[]{:S(2)}) copy-start(bf16[1,12,32,1024]{3,2,1,0:T(8,128)(2,1)} %param.11) | copy-start | bytes 2359300
  161.2 3.0 copy-start.4
  161.2 3.0 copy-start.11
  166.2 3.1 copy-start.25
  166.2 3.1 copy-start.24
  177.6 4.3 %copy-start.23 = (bf16[1,1024,512]{2,1,0:T(8,128)(2,1)S(1)}, bf16[1,1024,512]{2,1,0:T(8,128)(2,1)}, u32[]{:S(2)}) copy-start(bf16[1,1024,512]{2,1,0:T(8,128)(2,1)} %all-gather.11.cloned.1.call-done) | copy-start | bytes 3145732
  177.6 4.3 %copy-start.26 = (bf16[12,8,128,64]{2,3,1,0:T(8,128)(2,1)S(1)}, bf16[12,8,128,64]{2,3,1,0:T(8,128)(2,1)}, u32[]{:S(2)}) copy-start(bf16[12,8,128,64]{2,3,1,0:T(8,128)(2,1)} %copy-done.25) | copy-start | bytes 4718596
  194.8 124.2 %all-to-all-start.2 = ((bf16[8,2,128,1024]{3,2,1,0:T(8,128)(2,1)}), bf16[8,2,128,1024]{3,2,1,0:T(8,128)(2,1)}, u32[]{:S(2)}, u32[]{:S(2)}) async-start(bf16[8,2,128,1024]{3,2,1,0:T(8,128)(2,1)} %broadcast_select_fusion), calls=%async_computation.2 | async-start | bytes 8388608 | tf_op jit(solution)/shard_map/all_to_all | solution.py:129
  199.6 115.1 %all-gather.15.cloned.1.call-start = ((), (), s32[]{:S(2)}) async-start(), calls=%async_computation.7 | async-start | bytes 5242880 | tf_op jit(solution)/shard_map/all_gather | solution.py:137
  207.7 12.7 %copy-start.10 = (bf16[1,12,32,1024]{3,2,1,0:T(8,128)(2,1)S(1)}, bf16[1,12,32,1024]{3,2,1,0:T(8,128)(2,1)}, u32[]{:S(2)}) copy-start(bf16[1,12,32,1024]{3,2,1,0:T(8,128)(2,1)} %param.11) | copy-start | bytes 2359300
  319.0 4.2 %copy-start.1 = (bf16[1,6,128,1024]{3,2,1,0:T(8,128)(2,1)S(1)}, bf16[1,6,128,1024]{3,2,1,0:T(8,128)(2,1)}, u32[]{:S(2)}) copy-start(bf16[1,6,128,1024]{3,2,1,0:T(8,128)(2,1)} %param.12) | copy-start | bytes 4718596
  (14 other events, 22.5 us)
Sparse Core Ops, SparseCore 0:
  32.2 27.9 all-gather.8
  62.0 26.4 all-gather.12
  90.4 26.4 all-gather.10
  118.6 26.4 all-gather.6
  172.6 87.1 all-reduce.2
  262.1 52.5 all-gather.14
